TPU v7x, 512 devices: a whole 4x4x16 slice. The times are simulated.
512 devices in a mesh: row: 4 (over x), col: 8 (over y, core), layer: 16 (over z).
Axes of the slice: x: 4, y: 4, z: 16, core: 2. Of those that a mesh axis runs over, the one named last changes fastest.
Arguments:
- a_blocks: bfloat16 [16, 2, 64, 64, 512], P('layer', None, ('row', 'col')), may hold values from -0.046875 to 0.046875
- a_cols: int32 [16, 2, 64, 8], P('layer', None, ('row', 'col')), may hold values from 0 to 7
- p_blocks: bfloat16 [16, 2, 8, 8, 64, 256], P('layer', None, 'col', 'row'), may hold values from -12 to 12
- p_cols: int32 [16, 2, 8, 8, 4], P('layer', None, 'col', 'row'), may hold values from 0 to 15, as said below
- c_cols: int32 [8, 64, 8], P('col', 'row'), may hold values from 0 to 15, as said below
Outputs:
- c_blocks: bfloat16 [8, 64, 64, 512], P('col', ('row', 'layer'))
Inputs may be any that keep to these rules, and one draw needn't show every extreme that they name: `p_cols`: the 4 entries of a block row of P in one column group are distinct. `c_cols`: the 8 entries of a block row of C in one column group are distinct.
All inputs are finite; a program needn't handle non-finite values.
Results may differ from a plain program's by a relative error of at most 0.008.
Values may be sent and summed in bfloat16 or wider, within the bound.
No kernel may reach another device: no remote copies, remote signals or barrier semaphores. Data moves between devices by JAX's collectives and lax.ppermute only.
A program may use at most 64 MiB of HBM per device.

v0:
```python
import jax
import jax.numpy as jnp
from jax import lax
from jax.experimental import pallas as pl
from jax.experimental.pallas import tpu as pltpu
from jax.sharding import PartitionSpec as P


BLK = 64
KS = 8
KP = 4
KC = 8
NCC = 16
SEC = 2
OWN = 2
IBS = 8
CORES = 2
HEAD = 16
BODY = SEC * OWN * BLK
PAIR = 2 * BLK
SMALL = 8 * 1024 * 1024
SHIFTS = ((0, 3), (2, 1))
HALF = 2
STEP = 16
VMEM = pl.BlockSpec(memory_space=pltpu.VMEM)
SMEM = pl.BlockSpec(memory_space=pltpu.SMEM)
HBM = pl.BlockSpec(memory_space=pltpu.HBM)


def head_row(values):
    lane = lax.broadcasted_iota(jnp.int32, (HEAD, PAIR), 1)
    row = jnp.zeros((HEAD, PAIR), jnp.float32)
    for n, value in enumerate(values):
        row = jnp.where(lane == n, value.astype(jnp.float32), row)
    return row.astype(jnp.bfloat16)


def pack_kernel(a_cols, p_cols, a_blocks, p_blocks, a_out, p_out):
    a_head = head_row([a_cols[0, s, j, k] for s in range(SEC) for j in range(OWN) for k in range(KS)])
    p_head = head_row([p_cols[0, s, 0, j, q] for s in range(SEC) for j in range(OWN) for q in range(KP)])
    for n in range(a_out.shape[0]):
        a_out[n, :BODY, :] = a_blocks[...]
        a_out[n, BODY:, :] = jnp.zeros((HEAD, KS * BLK), jnp.bfloat16)
        a_out[n, BODY:, :PAIR] = a_head
    p_out[:BODY, :] = p_blocks[...]
    p_out[BODY:, :] = jnp.zeros((HEAD, KP * BLK), jnp.bfloat16)
    p_out[BODY:, :PAIR] = p_head


def twins(two):
    turned = pltpu.roll(two, BLK, 1)
    low = lax.broadcasted_iota(jnp.int32, two.shape, 1) < BLK
    return jnp.where(low, two, turned), jnp.where(low, turned, two)


def copies_of(tile):
    found = []
    for t in range(tile.shape[1] // PAIR):
        found.extend(twins(tile[:, t * PAIR : (t + 1) * PAIR].astype(jnp.float32)))
    return found


def swap(tile):
    return jnp.concatenate([tile[:, BLK:], tile[:, :BLK]], axis=1)


def masks_of(head, first, count, pairs):
    half = lax.broadcasted_iota(jnp.int32, (STEP, PAIR), 1) // BLK
    cols = [jnp.broadcast_to(head[:, first + n : first + n + 1], (STEP, PAIR)) for n in range(count)]
    return [[(half + 2 * pair).astype(jnp.float32) == col for col in cols] for pair in pairs]


def source_of(shift, axis):
    size = lax.axis_size(axis)
    return lax.rem(lax.axis_index(axis) - shift + size, size)


def expand_kernel(*refs):
    p_parts, (wide, held, sems) = refs[:HALF], refs[HALF:]
    copies = [pltpu.make_async_copy(part, held.at[n], sems.at[n]) for n, part in enumerate(p_parts)]
    for copy in copies:
        copy.start()
    for place, copy in enumerate(copies):
        copy.wait()
        head = held[place, BODY:, :PAIR].astype(jnp.float32)
        for n in range(SEC * OWN):
            s, j = n // OWN, n % OWN
            masks = masks_of(head, n * KP, KP, range(NCC // 2))
            slab = ((s * HALF + place) * OWN + j) * BLK
            for g in range(BLK // STEP):
                copies_in = copies_of(held[place, n * BLK + g * STEP : n * BLK + (g + 1) * STEP, :])
                for pair in range(NCC // 2):
                    acc = jnp.where(masks[pair][0], copies_in[0], 0.0)
                    for q in range(1, KP):
                        acc = jnp.where(masks[pair][q], copies_in[q], acc)
                    first = slab + g * STEP
                    wide[first : first + STEP, pair * PAIR : (pair + 1) * PAIR] = acc.astype(jnp.bfloat16)


def gather_rows(a_ref, rows):
    sources = [source_of(shift, "row") for shifts in SHIFTS for shift in shifts]
    for src in range(a_ref.shape[0]):
        head = a_ref[src, BODY:, :PAIR].astype(jnp.float32)
        for j in range(OWN):
            row = src * BLK
            for s in range(SEC):
                masks = masks_of(head, (s * OWN + j) * KS, KS, sources)
                for g in range(BLK // STEP):
                    first = (s * OWN + j) * BLK + g * STEP
                    copies = copies_of(a_ref[src, first : first + STEP, :])
                    for pair in range(IBS // OWN):
                        acc = jnp.where(masks[pair][0], copies[0], 0.0)
                        for k in range(1, KS):
                            acc = acc + jnp.where(masks[pair][k], copies[k], 0.0)
                        lane = ((pair // HALF * SEC + s) * HALF + pair % HALF) * PAIR
                        rows[j, row + g * STEP : row + (g + 1) * STEP, lane : lane + PAIR] = acc.astype(jnp.bfloat16)


def all_rows(rows_own, a_other, rows):
    rows[0] = rows_own[...]
    gather_rows(a_other, rows.at[1])


def product_kernel(near, turn, c_cols, rows, wide_first, wide_second, out, full):
    core, layer = lax.axis_index("core"), lax.axis_index("layer")
    place = lax.rem(layer, near) ^ turn
    owner, j = place // OWN, lax.rem(place, OWN)
    side = jnp.where(owner == core, 0, 1)
    wide = jnp.concatenate([wide_first[...], wide_second[...]], axis=0)
    full[...] = jnp.dot(rows[side, j], wide, preferred_element_type=jnp.float32).astype(jnp.bfloat16)
    low = lax.broadcasted_iota(jnp.int32, (BLK, PAIR), 1).astype(jnp.int16) < jnp.int16(BLK)
    for n in range(out.shape[0]):
        i = n * near + place
        for pair in range(KC // 2):
            picked = []
            for m in range(2):
                c = c_cols[0, pair * 2 + m, i]
                two = full[n * BLK : (n + 1) * BLK, pl.ds(pl.multiple_of(c // 2 * PAIR, PAIR), PAIR)]
                picked.append(jnp.where(lax.rem(c, 2) == m, two, swap(two)))
            out[n, :, pair * PAIR : (pair + 1) * PAIR] = jnp.where(low, *picked)


def local(a_blocks, a_cols, p_blocks, p_cols, c_cols):
    rows, chips, layers = lax.axis_size("row"), lax.axis_size("chip"), lax.axis_size("layer")
    near = 4
    a_out, p_out = pl.pallas_call(
        pack_kernel,
        out_shape=(
            jax.ShapeDtypeStruct((chips, BODY + HEAD, KS * BLK), jnp.bfloat16),
            jax.ShapeDtypeStruct((BODY + HEAD, KP * BLK), jnp.bfloat16),
        ),
        in_specs=[SMEM, SMEM, VMEM, VMEM],
        out_specs=(VMEM, VMEM),
    )(a_cols, p_cols, a_blocks.reshape(BODY, KS * BLK), p_blocks.reshape(BODY, KP * BLK))

    def expand(*parts):
        return pl.pallas_call(
            expand_kernel,
            out_shape=jax.ShapeDtypeStruct((HALF * SEC * OWN * BLK, NCC * BLK), jnp.bfloat16),
            in_specs=[HBM] * HALF,
            out_specs=VMEM,
            scratch_shapes=[
                pltpu.VMEM((HALF, BODY + HEAD, KP * BLK), jnp.bfloat16),
                pltpu.SemaphoreType.DMA((HALF,)),
            ],
            cost_estimate=pl.CostEstimate(flops=10**6, bytes_accessed=2 * 10**6, transcendentals=0),
            compiler_params=pltpu.CompilerParams(vmem_limit_bytes=SMALL),
        )(*parts)

    a_own = lax.all_to_all(a_out, "chip", 0, 0, tiled=True)
    p_parts = [p_out] + [lax.ppermute(p_out, "row", [(i, (i + d) % rows) for i in range(rows)]) for d in range(1, rows)]
    first = expand(*[p_parts[d] for d in SHIFTS[0]])
    a_other = lax.ppermute(a_own, "core", [(0, 1), (1, 0)])
    rows_own = pl.pallas_call(
        gather_rows,
        out_shape=jax.ShapeDtypeStruct((OWN, chips * BLK, SEC * IBS * BLK), jnp.bfloat16),
        in_specs=[VMEM],
        out_specs=VMEM,
        cost_estimate=pl.CostEstimate(flops=10**6, bytes_accessed=2 * 10**6, transcendentals=0),
        compiler_params=pltpu.CompilerParams(vmem_limit_bytes=SMALL),
    )(a_own)
    second = expand(*[p_parts[d] for d in SHIFTS[1]])
    rows_all = pl.pallas_call(
        all_rows,
        out_shape=jax.ShapeDtypeStruct((CORES,) + rows_own.shape, jnp.bfloat16),
        in_specs=[VMEM, VMEM],
        out_specs=VMEM,
        cost_estimate=pl.CostEstimate(flops=10**6, bytes_accessed=4 * 10**6, transcendentals=0),
        compiler_params=pltpu.CompilerParams(vmem_limit_bytes=SMALL),
    )(rows_own, a_other)

    def product(turn):
        return pl.pallas_call(
            lambda *refs: product_kernel(near, turn, *refs),
            out_shape=jax.ShapeDtypeStruct((layers // near, BLK, KC * BLK), jnp.bfloat16),
            in_specs=[SMEM] + [VMEM] * 3,
            out_specs=VMEM,
            scratch_shapes=[pltpu.VMEM((chips * BLK, NCC * BLK), jnp.bfloat16)],
            cost_estimate=pl.CostEstimate(flops=5 * 10**8, bytes_accessed=3 * 10**6, transcendentals=0),
            compiler_params=pltpu.CompilerParams(vmem_limit_bytes=2 * SMALL),
        )(c_cols.transpose(0, 2, 1), rows_all, first, second)

    def partners(turn):
        pairs = []
        for core in range(CORES):
            for n in range(layers):
                start = near // 2 * core
                to = n // near * near + (n % near ^ turn)
                pairs.append((core * layers + (n + start) % layers, core * layers + (to + start) % layers))
        return pairs

    sums = []
    for turn in range(near - 1, 0, -1):
        sent = product(turn)
        sums.append(lax.ppermute(sent, ("core", "layer"), partners(turn)))
    sums.append(product(0))
    part = sum(v.astype(jnp.float32) for v in sums).astype(jnp.bfloat16)
    far = [[o + near * g for g in range(layers // near)] for o in range(near)]
    got = lax.all_to_all(part, "layer", 0, 0, axis_index_groups=far, tiled=True)
    return got.astype(jnp.float32).sum(axis=0).astype(jnp.bfloat16)[None, None]


def solution(mesh):
    rows, cols, layers = mesh.devices.shape
    split = jax.sharding.Mesh(
        mesh.devices.reshape(rows, cols // CORES, CORES, layers), ("row", "chip", "core", "layer")
    )
    col = ("chip", "core")
    return jax.shard_map(
        local,
        mesh=split,
        in_specs=(
            P("layer", None, ("row",) + col, None, None),
            P("layer", None, ("row",) + col, None),
            P("layer", None, col, "row", None, None),
            P("layer", None, col, "row", None),
            P(col, "row", None),
        ),
        out_specs=P(col, ("row", "layer"), None, None),
        check_vma=False,
    )
```

profile of v0, /device:TPU:33, one launch (start us, length us, event | category | flops | bytes accessed | tf_op | source)
XLA Modules:
  0.0 106.7 jit_solution(12846249570003651059)
XLA Ops:
  0.0 2.1 %shard_map.55 = (bf16[4,272,512]{2,1,0:T(8,128)(2,1)}, bf16[272,256]{1,0:T(8,128)(2,1)}) custom-call(s32[1,2,2,8]{3,2,1,0:T(2,128)} %a_cols.1, s32[1,2,1,2,4]{4,3,2,1,0:T(2,128)} %p_cols.1, bf16[256,512]{1,0:T(8,128)(2,1)} %bitcast.8, bf16[256,256]{1,0:T(8,128)(2,1)} %bitcast.9), custom_call_target="tpu_custom_call" | custom-call | tf_op jit(solution)/shard_map/pallas_call | solution.py:146
  2.1 0.0 copy-start
  2.1 19.0 %all_to_all.10.a_ref = bf16[4,272,512]{2,1,0:T(8,128)(2,1)S(1)} all-to-all(bf16[4,272,512]{2,1,0:T(8,128)(2,1)} %get-tuple-element.7), channel_id=1, replica_groups=mesh['row'=4,'chip'=4,'core'=2,'layer'=16] {'chip'}, dimensions={0} | all-to-all | bytes 2228224 | tf_op jit(solution)/shard_map/all_to_all | solution.py:170
  21.1 4.0 %collective-permute-start = (bf16[4,272,512]{2,1,0:T(8,128)(2,1)S(1)}, bf16[4,272,512]{2,1,0:T(8,128)(2,1)S(1)}, u32[]{:S(2)}, u32[]{:S(2)}) collective-permute-start(bf16[4,272,512]{2,1,0:T(8,128)(2,1)S(1)} %all_to_all.10.a_ref), channel_id=1, source_target_pairs={{0,16},{16,0},{1,17},{17,1},{2,18},{18,2},{3,19},{19,3},{4,20},{20... | collective-permute-start | bytes 3342344 | tf_op jit(solution)/shard_map/ppermute | solution.py:173
  25.1 0.0 copy-done
  25.1 4.4 %collective-permute-start.1 = (bf16[272,256]{1,0:T(8,128)(2,1)S(1)}, bf16[272,256]{1,0:T(8,128)(2,1)S(1)}, u32[]{:S(2)}, u32[]{:S(2)}) collective-permute-start(bf16[272,256]{1,0:T(8,128)(2,1)S(1)} %copy-done), channel_id=1, source_target_pairs={{0,384},{128,0},{256,128},{384,256},{1,385},{129,1},{257,129},{385... | collective-permute-start | bytes 417800 | tf_op jit(solution)/shard_map/ppermute | solution.py:171
  29.5 2.4 %collective-permute-start.2 = (bf16[272,256]{1,0:T(8,128)(2,1)S(1)}, bf16[272,256]{1,0:T(8,128)(2,1)S(1)}, u32[]{:S(2)}, u32[]{:S(2)}) collective-permute-start(bf16[272,256]{1,0:T(8,128)(2,1)S(1)} %copy-done), channel_id=1, source_target_pairs={{0,256},{128,384},{256,0},{384,128},{1,257},{129,385},{257,1},{385... | collective-permute-start | bytes 417800 | tf_op jit(solution)/shard_map/ppermute | solution.py:171
  31.9 2.5 %collective-permute-start.3 = (bf16[272,256]{1,0:T(8,128)(2,1)S(1)}, bf16[272,256]{1,0:T(8,128)(2,1)S(1)}, u32[]{:S(2)}, u32[]{:S(2)}) collective-permute-start(bf16[272,256]{1,0:T(8,128)(2,1)S(1)} %copy-done), channel_id=1, source_target_pairs={{0,128},{128,256},{256,384},{384,0},{1,129},{129,257},{257,385},{3... | collective-permute-start | bytes 417800 | tf_op jit(solution)/shard_map/ppermute | solution.py:171
  34.5 0.0 collective-permute-done.1.refs_1_
  34.5 1.2 %shard_map.58.refs_2_ = bf16[512,1024]{1,0:T(8,128)(2,1)S(1)} custom-call(bf16[272,256]{1,0:T(8,128)(2,1)S(1)} %copy-done, bf16[272,256]{1,0:T(8,128)(2,1)S(1)} %collective-permute-done.1.refs_1_), custom_call_target="tpu_custom_call" | custom-call | flops 1000000 | bytes 2000000 | tf_op jit(solution)/shard_map/pallas_call | solution.py:157
  35.7 2.2 %collective-permute-done.2.refs_0_ = bf16[272,256]{1,0:T(8,128)(2,1)S(1)} collective-permute-done((bf16[272,256]{1,0:T(8,128)(2,1)S(1)}, bf16[272,256]{1,0:T(8,128)(2,1)S(1)}, u32[]{:S(2)}, u32[]{:S(2)}) %collective-permute-start.2) | collective-permute-done | bytes 139296 | tf_op jit(solution)/shard_map/ppermute | solution.py:171
  37.8 3.3 %collective-permute-done.3.refs_1_ = bf16[272,256]{1,0:T(8,128)(2,1)S(1)} collective-permute-done((bf16[272,256]{1,0:T(8,128)(2,1)S(1)}, bf16[272,256]{1,0:T(8,128)(2,1)S(1)}, u32[]{:S(2)}, u32[]{:S(2)}) %collective-permute-start.3) | collective-permute-done | bytes 139296 | tf_op jit(solution)/shard_map/ppermute | solution.py:171
  41.1 1.1 %shard_map.59.refs_3_ = bf16[512,1024]{1,0:T(8,128)(2,1)S(1)} custom-call(bf16[272,256]{1,0:T(8,128)(2,1)S(1)} %collective-permute-done.2.refs_0_, bf16[272,256]{1,0:T(8,128)(2,1)S(1)} %collective-permute-done.3.refs_1_), custom_call_target="tpu_custom_call" | custom-call | flops 1000000 | bytes 2000000 | tf_op jit(solution)/shard_map/pallas_call | solution.py:157
  42.3 2.1 %shard_map.56.rows_own = bf16[2,256,1024]{2,1,0:T(8,128)(2,1)S(1)} custom-call(bf16[4,272,512]{2,1,0:T(8,128)(2,1)S(1)} %all_to_all.10.a_ref), custom_call_target="tpu_custom_call" | custom-call | flops 1000000 | bytes 2000000 | tf_op jit(solution)/shard_map/pallas_call | solution.py:174
  44.3 0.0 copy-start.1
  44.3 0.0 collective-permute-done.a_other
  44.4 2.1 %shard_map.57.refs_1_ = bf16[2,2,256,1024]{3,2,1,0:T(8,128)(2,1)S(1)} custom-call(bf16[2,256,1024]{2,1,0:T(8,128)(2,1)S(1)} %shard_map.56.rows_own, bf16[4,272,512]{2,1,0:T(8,128)(2,1)S(1)} %collective-permute-done.a_other), custom_call_target="tpu_custom_call" | custom-call | flops 1000000 | bytes 4000000 | tf_op jit(solution)/shard_map/pallas_call | solution.py:183
  46.4 0.0 copy-done.1
  46.5 1.6 %shard_map.62 = bf16[4,64,512]{2,1,0:T(8,128)(2,1)S(1)} custom-call(s32[1,8,16]{2,1,0:T(8,128)S(1)} %bitcast.4, bf16[2,2,256,1024]{3,2,1,0:T(8,128)(2,1)S(1)} %shard_map.57.refs_1_, bf16[512,1024]{1,0:T(8,128)(2,1)S(1)} %shard_map.58.refs_2_, bf16[512,1024]{1,0:T(8,128)(2,1)S(1)} %shard_map.59.refs_3_), custom_call_target="tpu_custom_call" | custom-call | flops 500000000 | bytes 3000000 | tf_op jit(solution)/shard_map/pallas_call | solution.py:193
  48.1 1.6 %shard_map.61 = bf16[4,64,512]{2,1,0:T(8,128)(2,1)S(1)} custom-call(s32[1,8,16]{2,1,0:T(8,128)S(1)} %bitcast.5, bf16[2,2,256,1024]{3,2,1,0:T(8,128)(2,1)S(1)} %shard_map.57.refs_1_, bf16[512,1024]{1,0:T(8,128)(2,1)S(1)} %shard_map.58.refs_2_, bf16[512,1024]{1,0:T(8,128)(2,1)S(1)} %shard_map.59.refs_3_), custom_call_target="tpu_custom_call" | custom-call | flops 500000000 | bytes 3000000 | tf_op jit(solution)/shard_map/pallas_call | solution.py:193
  49.7 1.6 %shard_map.60 = bf16[4,64,512]{2,1,0:T(8,128)(2,1)S(1)} custom-call(s32[1,8,16]{2,1,0:T(8,128)S(1)} %bitcast.6, bf16[2,2,256,1024]{3,2,1,0:T(8,128)(2,1)S(1)} %shard_map.57.refs_1_, bf16[512,1024]{1,0:T(8,128)(2,1)S(1)} %shard_map.58.refs_2_, bf16[512,1024]{1,0:T(8,128)(2,1)S(1)} %shard_map.59.refs_3_), custom_call_target="tpu_custom_call" | custom-call | flops 500000000 | bytes 3000000 | tf_op jit(solution)/shard_map/pallas_call | solution.py:193
  51.3 1.9 %collective-permute-start.6 = (bf16[4,64,512]{2,1,0:T(8,128)(2,1)S(1)}, bf16[4,64,512]{2,1,0:T(8,128)(2,1)S(1)}, u32[]{:S(2)}, u32[]{:S(2)}) collective-permute-start(bf16[4,64,512]{2,1,0:T(8,128)(2,1)S(1)} %shard_map.62), channel_id=1, source_target_pairs={{0,1},{1,0},{2,3},{3,2},{4,5},{5,4},{6,7},{7,6},{8,9},{9,8},{10,11... | collective-permute-start | bytes 786440 | tf_op jit(solution)/shard_map/ppermute | solution.py:215
  53.2 11.4 %collective-permute-start.5 = (bf16[4,64,512]{2,1,0:T(8,128)(2,1)S(1)}, bf16[4,64,512]{2,1,0:T(8,128)(2,1)S(1)}, u32[]{:S(2)}, u32[]{:S(2)}) collective-permute-start(bf16[4,64,512]{2,1,0:T(8,128)(2,1)S(1)} %shard_map.61), channel_id=1, source_target_pairs={{0,2},{1,3},{2,0},{3,1},{4,6},{5,7},{6,4},{7,5},{8,10},{9,11},{10,... | collective-permute-start | bytes 786440 | tf_op jit(solution)/shard_map/ppermute | solution.py:215
  64.6 2.4 %collective-permute-start.4 = (bf16[4,64,512]{2,1,0:T(8,128)(2,1)S(1)}, bf16[4,64,512]{2,1,0:T(8,128)(2,1)S(1)}, u32[]{:S(2)}, u32[]{:S(2)}) collective-permute-start(bf16[4,64,512]{2,1,0:T(8,128)(2,1)S(1)} %shard_map.60), channel_id=1, source_target_pairs={{0,3},{1,2},{2,1},{3,0},{4,7},{5,6},{6,5},{7,4},{8,11},{9,10},{10,... | collective-permute-start | bytes 786440 | tf_op jit(solution)/shard_map/ppermute | solution.py:215
  67.0 1.6 %shard_map.63 = bf16[4,64,512]{2,1,0:T(8,128)(2,1)S(1)} custom-call(s32[1,8,16]{2,1,0:T(8,128)S(1)} %bitcast.7, bf16[2,2,256,1024]{3,2,1,0:T(8,128)(2,1)S(1)} %shard_map.57.refs_1_, bf16[512,1024]{1,0:T(8,128)(2,1)S(1)} %shard_map.58.refs_2_, bf16[512,1024]{1,0:T(8,128)(2,1)S(1)} %shard_map.59.refs_3_), custom_call_target="tpu_custom_call" | custom-call | flops 500000000 | bytes 3000000 | tf_op jit(solution)/shard_map/pallas_call | solution.py:193
  68.6 0.0 collective-permute-done.6
  68.6 0.0 collective-permute-done.5
  68.6 12.4 %collective-permute-done.4 = bf16[4,64,512]{2,1,0:T(8,128)(2,1)S(1)} collective-permute-done((bf16[4,64,512]{2,1,0:T(8,128)(2,1)S(1)}, bf16[4,64,512]{2,1,0:T(8,128)(2,1)S(1)}, u32[]{:S(2)}, u32[]{:S(2)}) %collective-permute-start.4) | collective-permute-done | bytes 262176 | tf_op jit(solution)/shard_map/ppermute | solution.py:215
  80.9 0.1 add_convert_fusion
  81.1 25.0 %all_to_all.11 = bf16[4,64,512]{2,1,0:T(8,128)(2,1)S(1)} all-to-all(bf16[4,64,512]{2,1,0:T(8,128)(2,1)S(1)} %add_convert_fusion), channel_id=1, replica_groups={{0,4,8,12},{1,5,9,13},{2,6,10,14},{3,7,11,15},{16,20,24,28},{17,21,25,2..., dimensions={0} | all-to-all | bytes 524288 | tf_op jit(solution)/shard_map/all_to_all | solution.py:219
  106.1 0.7 reduce_sum.12
Async XLA Ops:
  2.1 23.0 %copy-start = (bf16[272,256]{1,0:T(8,128)(2,1)S(1)}, bf16[272,256]{1,0:T(8,128)(2,1)}, u32[]{:S(2)}) copy-start(bf16[272,256]{1,0:T(8,128)(2,1)} %get-tuple-element.8.refs_0_) | copy-start | bytes 417796
  21.1 23.3 %collective-permute-start = (bf16[4,272,512]{2,1,0:T(8,128)(2,1)S(1)}, bf16[4,272,512]{2,1,0:T(8,128)(2,1)S(1)}, u32[]{:S(2)}, u32[]{:S(2)}) collective-permute-start(bf16[4,272,512]{2,1,0:T(8,128)(2,1)S(1)} %all_to_all.10.a_ref), channel_id=1, source_target_pairs={{0,16},{16,0},{1,17},{17,1},{2,18},{18,2},{3,19},{19,3},{4,20},{20... | collective-permute-start | bytes 3342344 | tf_op jit(solution)/shard_map/ppermute | solution.py:173
  25.1 9.4 %collective-permute-start.1 = (bf16[272,256]{1,0:T(8,128)(2,1)S(1)}, bf16[272,256]{1,0:T(8,128)(2,1)S(1)}, u32[]{:S(2)}, u32[]{:S(2)}) collective-permute-start(bf16[272,256]{1,0:T(8,128)(2,1)S(1)} %copy-done), channel_id=1, source_target_pairs={{0,384},{128,0},{256,128},{384,256},{1,385},{129,1},{257,129},{385... | collective-permute-start | bytes 417800 | tf_op jit(solution)/shard_map/ppermute | solution.py:171
  29.5 8.3 %collective-permute-start.2 = (bf16[272,256]{1,0:T(8,128)(2,1)S(1)}, bf16[272,256]{1,0:T(8,128)(2,1)S(1)}, u32[]{:S(2)}, u32[]{:S(2)}) collective-permute-start(bf16[272,256]{1,0:T(8,128)(2,1)S(1)} %copy-done), channel_id=1, source_target_pairs={{0,256},{128,384},{256,0},{384,128},{1,257},{129,385},{257,1},{385... | collective-permute-start | bytes 417800 | tf_op jit(solution)/shard_map/ppermute | solution.py:171
  31.9 9.2 %collective-permute-start.3 = (bf16[272,256]{1,0:T(8,128)(2,1)S(1)}, bf16[272,256]{1,0:T(8,128)(2,1)S(1)}, u32[]{:S(2)}, u32[]{:S(2)}) collective-permute-start(bf16[272,256]{1,0:T(8,128)(2,1)S(1)} %copy-done), channel_id=1, source_target_pairs={{0,128},{128,256},{256,384},{384,0},{1,129},{129,257},{257,385},{3... | collective-permute-start | bytes 417800 | tf_op jit(solution)/shard_map/ppermute | solution.py:171
  44.3 2.1 %copy-start.1 = (s32[1,16,8]{1,2,0:T(8,128)S(1)}, s32[1,16,8]{1,2,0:T(8,128)}, u32[]{:S(2)}) copy-start(s32[1,16,8]{1,2,0:T(8,128)} %param.9) | copy-start | bytes 1540
  51.3 17.3 %collective-permute-start.6 = (bf16[4,64,512]{2,1,0:T(8,128)(2,1)S(1)}, bf16[4,64,512]{2,1,0:T(8,128)(2,1)S(1)}, u32[]{:S(2)}, u32[]{:S(2)}) collective-permute-start(bf16[4,64,512]{2,1,0:T(8,128)(2,1)S(1)} %shard_map.62), channel_id=1, source_target_pairs={{0,1},{1,0},{2,3},{3,2},{4,5},{5,4},{6,7},{7,6},{8,9},{9,8},{10,11... | collective-permute-start | bytes 786440 | tf_op jit(solution)/shard_map/ppermute | solution.py:215
  53.2 15.4 %collective-permute-start.5 = (bf16[4,64,512]{2,1,0:T(8,128)(2,1)S(1)}, bf16[4,64,512]{2,1,0:T(8,128)(2,1)S(1)}, u32[]{:S(2)}, u32[]{:S(2)}) collective-permute-start(bf16[4,64,512]{2,1,0:T(8,128)(2,1)S(1)} %shard_map.61), channel_id=1, source_target_pairs={{0,2},{1,3},{2,0},{3,1},{4,6},{5,7},{6,4},{7,5},{8,10},{9,11},{10,... | collective-permute-start | bytes 786440 | tf_op jit(solution)/shard_map/ppermute | solution.py:215
  64.6 16.4 %collective-permute-start.4 = (bf16[4,64,512]{2,1,0:T(8,128)(2,1)S(1)}, bf16[4,64,512]{2,1,0:T(8,128)(2,1)S(1)}, u32[]{:S(2)}, u32[]{:S(2)}) collective-permute-start(bf16[4,64,512]{2,1,0:T(8,128)(2,1)S(1)} %shard_map.60), channel_id=1, source_target_pairs={{0,3},{1,2},{2,1},{3,0},{4,7},{5,6},{6,5},{7,4},{8,11},{9,10},{10,... | collective-permute-start | bytes 786440 | tf_op jit(solution)/shard_map/ppermute | solution.py:215
where the time goes:
time: 107 us
  blocking collectives  44 us (41%)
  starting transfers between devices  29 us (27%)
  waiting for transfers between devices  17.8 us (17%)
  Pallas kernels  15 us (14%)
    all_to_all x1, blocking collectives, local(): got = lax.all_to_all(part, 'layer', 0, 0, axis_index_groups=far, tiled=True)  25 us
    all_to_all x1, blocking collectives, local(): a_own = lax.all_to_all(a_out, 'chip', 0, 0, tiled=True)  19 us
    ppermute x3, starting transfers between devices, local(): sums.append(lax.ppermute(sent, ('core', 'layer'), partners(turn)))  15.7 us
    ppermute x3, waiting for transfers between devices, local(): sums.append(lax.ppermute(sent, ('core', 'layer'), partners(turn)))  12.4 us
    ppermute x3, starting transfers between devices, local(): lax.ppermute(p_out, 'row', [(i, (i + d) % rows) for i in range(rows)])  9.33 us
    pallas_call x4, Pallas kernels, product(): pl.pallas_call(lambda *refs: product_kernel(near, turn, *refs), out_shape...  6.36 us
    ppermute x3, waiting for transfers between devices, local(): lax.ppermute(p_out, 'row', [(i, (i + d) % rows) for i in range(rows)])  5.46 us
    ppermute x1, starting transfers between devices, local(): a_other = lax.ppermute(a_own, 'core', [(0, 1), (1, 0)])  4 us
  transfers between devices with their start and end apart: 7, of which 3 were waited for; matrix products, arithmetic and copies ran while one was open for 0% of the time, Pallas kernels for 6%

commit v1 on v0

--- a/solution.py
+++ b/solution.py
@@ -35,16 +35,19 @@
     return row.astype(jnp.bfloat16)
 
 
-def pack_kernel(a_cols, p_cols, a_blocks, p_blocks, a_out, p_out):
-    a_head = head_row([a_cols[0, s, j, k] for s in range(SEC) for j in range(OWN) for k in range(KS)])
-    p_head = head_row([p_cols[0, s, 0, j, q] for s in range(SEC) for j in range(OWN) for q in range(KP)])
+def pack_a_kernel(a_cols, a_blocks, a_out):
+    head = head_row([a_cols[0, s, j, k] for s in range(SEC) for j in range(OWN) for k in range(KS)])
     for n in range(a_out.shape[0]):
         a_out[n, :BODY, :] = a_blocks[...]
         a_out[n, BODY:, :] = jnp.zeros((HEAD, KS * BLK), jnp.bfloat16)
-        a_out[n, BODY:, :PAIR] = a_head
+        a_out[n, BODY:, :PAIR] = head
+
+
+def pack_p_kernel(p_cols, p_blocks, p_out):
+    head = head_row([p_cols[0, s, 0, j, q] for s in range(SEC) for j in range(OWN) for q in range(KP)])
     p_out[:BODY, :] = p_blocks[...]
     p_out[BODY:, :] = jnp.zeros((HEAD, KP * BLK), jnp.bfloat16)
-    p_out[BODY:, :PAIR] = p_head
+    p_out[BODY:, :PAIR] = head
 
 
 def twins(two):
@@ -99,21 +102,30 @@
 
 def gather_rows(a_ref, rows):
     sources = [source_of(shift, "row") for shifts in SHIFTS for shift in shifts]
+    half = lax.broadcasted_iota(jnp.int32, (STEP, PAIR), 1) // BLK
+    low = half.astype(jnp.int16) < jnp.int16(1)
+    none = jnp.zeros((STEP, PAIR), jnp.bfloat16)
     for src in range(a_ref.shape[0]):
         head = a_ref[src, BODY:, :PAIR].astype(jnp.float32)
         for j in range(OWN):
             row = src * BLK
             for s in range(SEC):
-                masks = masks_of(head, (s * OWN + j) * KS, KS, sources)
+                at = (s * OWN + j) * KS
+                cols = [jnp.broadcast_to(head[:, at + k : at + k + 1], (STEP, PAIR)) for k in range(KS)]
+                cols = [col.astype(jnp.int32).astype(jnp.int16) for col in cols]
+                masks = [[(half + 2 * pair).astype(jnp.int16) == col for col in cols] for pair in sources]
                 for g in range(BLK // STEP):
                     first = (s * OWN + j) * BLK + g * STEP
-                    copies = copies_of(a_ref[src, first : first + STEP, :])
+                    copies = []
+                    for t in range(KS // 2):
+                        two = a_ref[src, first : first + STEP, t * PAIR : (t + 1) * PAIR]
+                        copies += [jnp.where(low, two, swap(two)), jnp.where(low, swap(two), two)]
                     for pair in range(IBS // OWN):
-                        acc = jnp.where(masks[pair][0], copies[0], 0.0)
+                        acc = jnp.where(masks[pair][0], copies[0], none)
                         for k in range(1, KS):
-                            acc = acc + jnp.where(masks[pair][k], copies[k], 0.0)
+                            acc = acc + jnp.where(masks[pair][k], copies[k], none)
                         lane = ((pair // HALF * SEC + s) * HALF + pair % HALF) * PAIR
-                        rows[j, row + g * STEP : row + (g + 1) * STEP, lane : lane + PAIR] = acc.astype(jnp.bfloat16)
+                        rows[j, row + g * STEP : row + (g + 1) * STEP, lane : lane + PAIR] = acc
 
 
 def all_rows(rows_own, a_other, rows):
@@ -143,15 +155,18 @@
 def local(a_blocks, a_cols, p_blocks, p_cols, c_cols):
     rows, chips, layers = lax.axis_size("row"), lax.axis_size("chip"), lax.axis_size("layer")
     near = 4
-    a_out, p_out = pl.pallas_call(
-        pack_kernel,
-        out_shape=(
-            jax.ShapeDtypeStruct((chips, BODY + HEAD, KS * BLK), jnp.bfloat16),
-            jax.ShapeDtypeStruct((BODY + HEAD, KP * BLK), jnp.bfloat16),
-        ),
-        in_specs=[SMEM, SMEM, VMEM, VMEM],
-        out_specs=(VMEM, VMEM),
-    )(a_cols, p_cols, a_blocks.reshape(BODY, KS * BLK), p_blocks.reshape(BODY, KP * BLK))
+    a_out = pl.pallas_call(
+        pack_a_kernel,
+        out_shape=jax.ShapeDtypeStruct((chips, BODY + HEAD, KS * BLK), jnp.bfloat16),
+        in_specs=[SMEM, VMEM],
+        out_specs=VMEM,
+    )(a_cols, a_blocks.reshape(BODY, KS * BLK))
+    p_out = pl.pallas_call(
+        pack_p_kernel,
+        out_shape=jax.ShapeDtypeStruct((BODY + HEAD, KP * BLK), jnp.bfloat16),
+        in_specs=[SMEM, VMEM],
+        out_specs=VMEM,
+    )(p_cols, p_blocks.reshape(BODY, KP * BLK))
 
     def expand(*parts):
         return pl.pallas_call(

time: 107 us -> 107 us (level)
    pallas_call x1 -> x2, Pallas kernels: 2.12 us -> 3.61 us  [the longest x1 2.03 us: local(): pl.pallas_call(pack_a_kernel, out_shape=jax.ShapeDtypeStruct((chips, BODY...]
where the time goes in v1:
time: 107 us; the launch traced here: 106 us
  blocking collectives  43.8 us (41%)
  starting transfers between devices  29 us (27%)
  waiting for transfers between devices  17.2 us (16%)
  Pallas kernels  14.4 us (13%)
    all_to_all x1, blocking collectives, local(): got = lax.all_to_all(part, 'layer', 0, 0, axis_index_groups=far, tiled=True)  25 us
    all_to_all x1, blocking collectives, local(): a_own = lax.all_to_all(a_out, 'chip', 0, 0, tiled=True)  18.8 us
    ppermute x3, starting transfers between devices, local(): sums.append(lax.ppermute(sent, ('core', 'layer'), partners(turn)))  15.7 us
    ppermute x3, waiting for transfers between devices, local(): sums.append(lax.ppermute(sent, ('core', 'layer'), partners(turn)))  12.4 us
    ppermute x3, starting transfers between devices, local(): lax.ppermute(p_out, 'row', [(i, (i + d) % rows) for i in range(rows)])  9.32 us
    pallas_call x4, Pallas kernels, product(): pl.pallas_call(lambda *refs: product_kernel(near, turn, *refs), out_shape...  6.37 us
    ppermute x3, waiting for transfers between devices, local(): lax.ppermute(p_out, 'row', [(i, (i + d) % rows) for i in range(rows)])  4.79 us
    ppermute x1, starting transfers between devices, local(): a_other = lax.ppermute(a_own, 'core', [(0, 1), (1, 0)])  4 us
  transfers between devices with their start and end apart: 7, of which 3 were waited for; matrix products, arithmetic and copies ran while one was open for 0% of the time, Pallas kernels for 6%

profile of v1, /device:TPU:33, one launch (start us, length us, event | category | flops | bytes accessed | tf_op | source)
XLA Modules:
  0.0 106.3 jit_solution(4440114791180232846)
XLA Ops:
  0.0 2.0 %shard_map.55 = bf16[4,272,512]{2,1,0:T(8,128)(2,1)} custom-call(s32[1,2,2,8]{3,2,1,0:T(2,128)} %a_cols.1, bf16[256,512]{1,0:T(8,128)(2,1)} %bitcast.8), custom_call_target="tpu_custom_call" | custom-call | tf_op jit(solution)/shard_map/pallas_call | solution.py:158
  2.0 18.8 %all_to_all.10.a_ref = bf16[4,272,512]{2,1,0:T(8,128)(2,1)S(1)} all-to-all(bf16[4,272,512]{2,1,0:T(8,128)(2,1)} %shard_map.55), channel_id=1, replica_groups=mesh['row'=4,'chip'=4,'core'=2,'layer'=16] {'chip'}, dimensions={0} | all-to-all | bytes 2228224 | tf_op jit(solution)/shard_map/all_to_all | solution.py:185
  20.9 4.0 %collective-permute-start = (bf16[4,272,512]{2,1,0:T(8,128)(2,1)S(1)}, bf16[4,272,512]{2,1,0:T(8,128)(2,1)S(1)}, u32[]{:S(2)}, u32[]{:S(2)}) collective-permute-start(bf16[4,272,512]{2,1,0:T(8,128)(2,1)S(1)} %all_to_all.10.a_ref), channel_id=1, source_target_pairs={{0,16},{16,0},{1,17},{17,1},{2,18},{18,2},{3,19},{19,3},{4,20},{20... | collective-permute-start | bytes 3342344 | tf_op jit(solution)/shard_map/ppermute | solution.py:188
  24.9 1.6 %shard_map.58.refs_0_ = bf16[272,256]{1,0:T(8,128)(2,1)} custom-call(s32[1,2,1,2,4]{4,3,2,1,0:T(2,128)} %p_cols.1, bf16[256,256]{1,0:T(8,128)(2,1)} %bitcast.9), custom_call_target="tpu_custom_call" | custom-call | tf_op jit(solution)/shard_map/pallas_call | solution.py:164
  26.5 4.4 %collective-permute-start.1 = (bf16[272,256]{1,0:T(8,128)(2,1)}, bf16[272,256]{1,0:T(8,128)(2,1)S(1)}, u32[]{:S(2)}, u32[]{:S(2)}) collective-permute-start(bf16[272,256]{1,0:T(8,128)(2,1)} %shard_map.58.refs_0_), channel_id=1, source_target_pairs={{0,384},{128,0},{256,128},{384,256},{1,385},{129,1},{257,129},{385... | collective-permute-start | bytes 417800 | tf_op jit(solution)/shard_map/ppermute | solution.py:186
  30.8 2.4 %collective-permute-start.2 = (bf16[272,256]{1,0:T(8,128)(2,1)}, bf16[272,256]{1,0:T(8,128)(2,1)S(1)}, u32[]{:S(2)}, u32[]{:S(2)}) collective-permute-start(bf16[272,256]{1,0:T(8,128)(2,1)} %shard_map.58.refs_0_), channel_id=1, source_target_pairs={{0,256},{128,384},{256,0},{384,128},{1,257},{129,385},{257,1},{385... | collective-permute-start | bytes 417800 | tf_op jit(solution)/shard_map/ppermute | solution.py:186
  33.3 2.5 %collective-permute-start.3 = (bf16[272,256]{1,0:T(8,128)(2,1)}, bf16[272,256]{1,0:T(8,128)(2,1)S(1)}, u32[]{:S(2)}, u32[]{:S(2)}) collective-permute-start(bf16[272,256]{1,0:T(8,128)(2,1)} %shard_map.58.refs_0_), channel_id=1, source_target_pairs={{0,128},{128,256},{256,384},{384,0},{1,129},{129,257},{257,385},{3... | collective-permute-start | bytes 417800 | tf_op jit(solution)/shard_map/ppermute | solution.py:186
  35.8 0.0 collective-permute-done.1.refs_1_
  35.8 0.0 copy-start
  35.8 0.9 copy-done
  36.7 1.1 %shard_map.59.refs_2_ = bf16[512,1024]{1,0:T(8,128)(2,1)S(1)} custom-call(bf16[272,256]{1,0:T(8,128)(2,1)S(1)} %copy-done, bf16[272,256]{1,0:T(8,128)(2,1)S(1)} %collective-permute-done.1.refs_1_), custom_call_target="tpu_custom_call" | custom-call | flops 1000000 | bytes 2000000 | tf_op jit(solution)/shard_map/pallas_call | solution.py:172
  37.9 1.5 %collective-permute-done.2.refs_0_ = bf16[272,256]{1,0:T(8,128)(2,1)S(1)} collective-permute-done((bf16[272,256]{1,0:T(8,128)(2,1)}, bf16[272,256]{1,0:T(8,128)(2,1)S(1)}, u32[]{:S(2)}, u32[]{:S(2)}) %collective-permute-start.2) | collective-permute-done | bytes 139296 | tf_op jit(solution)/shard_map/ppermute | solution.py:186
  39.4 3.3 %collective-permute-done.3.refs_1_ = bf16[272,256]{1,0:T(8,128)(2,1)S(1)} collective-permute-done((bf16[272,256]{1,0:T(8,128)(2,1)}, bf16[272,256]{1,0:T(8,128)(2,1)S(1)}, u32[]{:S(2)}, u32[]{:S(2)}) %collective-permute-start.3) | collective-permute-done | bytes 139296 | tf_op jit(solution)/shard_map/ppermute | solution.py:186
  42.6 1.1 %shard_map.60.refs_3_ = bf16[512,1024]{1,0:T(8,128)(2,1)S(1)} custom-call(bf16[272,256]{1,0:T(8,128)(2,1)S(1)} %collective-permute-done.2.refs_0_, bf16[272,256]{1,0:T(8,128)(2,1)S(1)} %collective-permute-done.3.refs_1_), custom_call_target="tpu_custom_call" | custom-call | flops 1000000 | bytes 2000000 | tf_op jit(solution)/shard_map/pallas_call | solution.py:172
  43.8 1.1 shard_map.56.rows_own
  44.9 0.0 copy-start.1
  44.9 0.0 collective-permute-done.a_other
  44.9 1.1 %shard_map.57.refs_1_ = bf16[2,2,256,1024]{3,2,1,0:T(8,128)(2,1)S(1)} custom-call(bf16[2,256,1024]{2,1,0:T(8,128)(2,1)S(1)} %shard_map.56.rows_own, bf16[4,272,512]{2,1,0:T(8,128)(2,1)S(1)} %collective-permute-done.a_other), custom_call_target="tpu_custom_call" | custom-call | flops 1000000 | bytes 4000000 | tf_op jit(solution)/shard_map/pallas_call | solution.py:198
  46.0 0.0 copy-done.1
  46.0 1.6 %shard_map.63 = bf16[4,64,512]{2,1,0:T(8,128)(2,1)S(1)} custom-call(s32[1,8,16]{2,1,0:T(8,128)S(1)} %bitcast.4, bf16[2,2,256,1024]{3,2,1,0:T(8,128)(2,1)S(1)} %shard_map.57.refs_1_, bf16[512,1024]{1,0:T(8,128)(2,1)S(1)} %shard_map.59.refs_2_, bf16[512,1024]{1,0:T(8,128)(2,1)S(1)} %shard_map.60.refs_3_), custom_call_target="tpu_custom_call" | custom-call | flops 500000000 | bytes 3000000 | tf_op jit(solution)/shard_map/pallas_call | solution.py:208
  47.6 1.6 %shard_map.62 = bf16[4,64,512]{2,1,0:T(8,128)(2,1)S(1)} custom-call(s32[1,8,16]{2,1,0:T(8,128)S(1)} %bitcast.5, bf16[2,2,256,1024]{3,2,1,0:T(8,128)(2,1)S(1)} %shard_map.57.refs_1_, bf16[512,1024]{1,0:T(8,128)(2,1)S(1)} %shard_map.59.refs_2_, bf16[512,1024]{1,0:T(8,128)(2,1)S(1)} %shard_map.60.refs_3_), custom_call_target="tpu_custom_call" | custom-call | flops 500000000 | bytes 3000000 | tf_op jit(solution)/shard_map/pallas_call | solution.py:208
  49.2 1.6 %shard_map.61 = bf16[4,64,512]{2,1,0:T(8,128)(2,1)S(1)} custom-call(s32[1,8,16]{2,1,0:T(8,128)S(1)} %bitcast.6, bf16[2,2,256,1024]{3,2,1,0:T(8,128)(2,1)S(1)} %shard_map.57.refs_1_, bf16[512,1024]{1,0:T(8,128)(2,1)S(1)} %shard_map.59.refs_2_, bf16[512,1024]{1,0:T(8,128)(2,1)S(1)} %shard_map.60.refs_3_), custom_call_target="tpu_custom_call" | custom-call | flops 500000000 | bytes 3000000 | tf_op jit(solution)/shard_map/pallas_call | solution.py:208
  50.8 1.9 %collective-permute-start.6 = (bf16[4,64,512]{2,1,0:T(8,128)(2,1)S(1)}, bf16[4,64,512]{2,1,0:T(8,128)(2,1)S(1)}, u32[]{:S(2)}, u32[]{:S(2)}) collective-permute-start(bf16[4,64,512]{2,1,0:T(8,128)(2,1)S(1)} %shard_map.63), channel_id=1, source_target_pairs={{0,1},{1,0},{2,3},{3,2},{4,5},{5,4},{6,7},{7,6},{8,9},{9,8},{10,11... | collective-permute-start | bytes 786440 | tf_op jit(solution)/shard_map/ppermute | solution.py:230
  52.7 11.4 %collective-permute-start.5 = (bf16[4,64,512]{2,1,0:T(8,128)(2,1)S(1)}, bf16[4,64,512]{2,1,0:T(8,128)(2,1)S(1)}, u32[]{:S(2)}, u32[]{:S(2)}) collective-permute-start(bf16[4,64,512]{2,1,0:T(8,128)(2,1)S(1)} %shard_map.62), channel_id=1, source_target_pairs={{0,2},{1,3},{2,0},{3,1},{4,6},{5,7},{6,4},{7,5},{8,10},{9,11},{10,... | collective-permute-start | bytes 786440 | tf_op jit(solution)/shard_map/ppermute | solution.py:230
  64.1 2.4 %collective-permute-start.4 = (bf16[4,64,512]{2,1,0:T(8,128)(2,1)S(1)}, bf16[4,64,512]{2,1,0:T(8,128)(2,1)S(1)}, u32[]{:S(2)}, u32[]{:S(2)}) collective-permute-start(bf16[4,64,512]{2,1,0:T(8,128)(2,1)S(1)} %shard_map.61), channel_id=1, source_target_pairs={{0,3},{1,2},{2,1},{3,0},{4,7},{5,6},{6,5},{7,4},{8,11},{9,10},{10,... | collective-permute-start | bytes 786440 | tf_op jit(solution)/shard_map/ppermute | solution.py:230
  66.5 1.6 %shard_map.64 = bf16[4,64,512]{2,1,0:T(8,128)(2,1)S(1)} custom-call(s32[1,8,16]{2,1,0:T(8,128)S(1)} %bitcast.7, bf16[2,2,256,1024]{3,2,1,0:T(8,128)(2,1)S(1)} %shard_map.57.refs_1_, bf16[512,1024]{1,0:T(8,128)(2,1)S(1)} %shard_map.59.refs_2_, bf16[512,1024]{1,0:T(8,128)(2,1)S(1)} %shard_map.60.refs_3_), custom_call_target="tpu_custom_call" | custom-call | flops 500000000 | bytes 3000000 | tf_op jit(solution)/shard_map/pallas_call | solution.py:208
  68.1 0.0 collective-permute-done.6
  68.1 0.0 collective-permute-done.5
  68.1 12.4 %collective-permute-done.4 = bf16[4,64,512]{2,1,0:T(8,128)(2,1)S(1)} collective-permute-done((bf16[4,64,512]{2,1,0:T(8,128)(2,1)S(1)}, bf16[4,64,512]{2,1,0:T(8,128)(2,1)S(1)}, u32[]{:S(2)}, u32[]{:S(2)}) %collective-permute-start.4) | collective-permute-done | bytes 262176 | tf_op jit(solution)/shard_map/ppermute | solution.py:230
  80.5 0.1 add_convert_fusion
  80.6 25.0 %all_to_all.11 = bf16[4,64,512]{2,1,0:T(8,128)(2,1)S(1)} all-to-all(bf16[4,64,512]{2,1,0:T(8,128)(2,1)S(1)} %add_convert_fusion), channel_id=1, replica_groups={{0,4,8,12},{1,5,9,13},{2,6,10,14},{3,7,11,15},{16,20,24,28},{17,21,25,2..., dimensions={0} | all-to-all | bytes 524288 | tf_op jit(solution)/shard_map/all_to_all | solution.py:234
  105.6 0.7 reduce_sum.12
Async XLA Ops:
  20.9 24.0 %collective-permute-start = (bf16[4,272,512]{2,1,0:T(8,128)(2,1)S(1)}, bf16[4,272,512]{2,1,0:T(8,128)(2,1)S(1)}, u32[]{:S(2)}, u32[]{:S(2)}) collective-permute-start(bf16[4,272,512]{2,1,0:T(8,128)(2,1)S(1)} %all_to_all.10.a_ref), channel_id=1, source_target_pairs={{0,16},{16,0},{1,17},{17,1},{2,18},{18,2},{3,19},{19,3},{4,20},{20... | collective-permute-start | bytes 3342344 | tf_op jit(solution)/shard_map/ppermute | solution.py:188
  26.5 9.3 %collective-permute-start.1 = (bf16[272,256]{1,0:T(8,128)(2,1)}, bf16[272,256]{1,0:T(8,128)(2,1)S(1)}, u32[]{:S(2)}, u32[]{:S(2)}) collective-permute-start(bf16[272,256]{1,0:T(8,128)(2,1)} %shard_map.58.refs_0_), channel_id=1, source_target_pairs={{0,384},{128,0},{256,128},{384,256},{1,385},{129,1},{257,129},{385... | collective-permute-start | bytes 417800 | tf_op jit(solution)/shard_map/ppermute | solution.py:186
  30.8 8.5 %collective-permute-start.2 = (bf16[272,256]{1,0:T(8,128)(2,1)}, bf16[272,256]{1,0:T(8,128)(2,1)S(1)}, u32[]{:S(2)}, u32[]{:S(2)}) collective-permute-start(bf16[272,256]{1,0:T(8,128)(2,1)} %shard_map.58.refs_0_), channel_id=1, source_target_pairs={{0,256},{128,384},{256,0},{384,128},{1,257},{129,385},{257,1},{385... | collective-permute-start | bytes 417800 | tf_op jit(solution)/shard_map/ppermute | solution.py:186
  33.3 9.4 %collective-permute-start.3 = (bf16[272,256]{1,0:T(8,128)(2,1)}, bf16[272,256]{1,0:T(8,128)(2,1)S(1)}, u32[]{:S(2)}, u32[]{:S(2)}) collective-permute-start(bf16[272,256]{1,0:T(8,128)(2,1)} %shard_map.58.refs_0_), channel_id=1, source_target_pairs={{0,128},{128,256},{256,384},{384,0},{1,129},{129,257},{257,385},{3... | collective-permute-start | bytes 417800 | tf_op jit(solution)/shard_map/ppermute | solution.py:186
  35.8 0.9 copy-start
  44.9 1.1 %copy-start.1 = (s32[1,16,8]{1,2,0:T(8,128)S(1)}, s32[1,16,8]{1,2,0:T(8,128)}, u32[]{:S(2)}) copy-start(s32[1,16,8]{1,2,0:T(8,128)} %param.9) | copy-start | bytes 1540
  50.8 17.3 %collective-permute-start.6 = (bf16[4,64,512]{2,1,0:T(8,128)(2,1)S(1)}, bf16[4,64,512]{2,1,0:T(8,128)(2,1)S(1)}, u32[]{:S(2)}, u32[]{:S(2)}) collective-permute-start(bf16[4,64,512]{2,1,0:T(8,128)(2,1)S(1)} %shard_map.63), channel_id=1, source_target_pairs={{0,1},{1,0},{2,3},{3,2},{4,5},{5,4},{6,7},{7,6},{8,9},{9,8},{10,11... | collective-permute-start | bytes 786440 | tf_op jit(solution)/shard_map/ppermute | solution.py:230
  52.7 15.4 %collective-permute-start.5 = (bf16[4,64,512]{2,1,0:T(8,128)(2,1)S(1)}, bf16[4,64,512]{2,1,0:T(8,128)(2,1)S(1)}, u32[]{:S(2)}, u32[]{:S(2)}) collective-permute-start(bf16[4,64,512]{2,1,0:T(8,128)(2,1)S(1)} %shard_map.62), channel_id=1, source_target_pairs={{0,2},{1,3},{2,0},{3,1},{4,6},{5,7},{6,4},{7,5},{8,10},{9,11},{10,... | collective-permute-start | bytes 786440 | tf_op jit(solution)/shard_map/ppermute | solution.py:230
  64.1 16.4 %collective-permute-start.4 = (bf16[4,64,512]{2,1,0:T(8,128)(2,1)S(1)}, bf16[4,64,512]{2,1,0:T(8,128)(2,1)S(1)}, u32[]{:S(2)}, u32[]{:S(2)}) collective-permute-start(bf16[4,64,512]{2,1,0:T(8,128)(2,1)S(1)} %shard_map.61), channel_id=1, source_target_pairs={{0,3},{1,2},{2,1},{3,0},{4,7},{5,6},{6,5},{7,4},{8,11},{9,10},{10,... | collective-permute-start | bytes 786440 | tf_op jit(solution)/shard_map/ppermute | solution.py:230

commit v2 on v1

--- a/solution.py
+++ b/solution.py
@@ -50,27 +50,24 @@
     p_out[BODY:, :PAIR] = head
 
 
-def twins(two):
-    turned = pltpu.roll(two, BLK, 1)
-    low = lax.broadcasted_iota(jnp.int32, two.shape, 1) < BLK
-    return jnp.where(low, two, turned), jnp.where(low, turned, two)
+def swap(tile):
+    return jnp.concatenate([tile[:, BLK:], tile[:, :BLK]], axis=1)
 
 
 def copies_of(tile):
+    low = lax.broadcasted_iota(jnp.int32, (STEP, PAIR), 1).astype(jnp.int16) < jnp.int16(BLK)
     found = []
     for t in range(tile.shape[1] // PAIR):
-        found.extend(twins(tile[:, t * PAIR : (t + 1) * PAIR].astype(jnp.float32)))
+        two = tile[:, t * PAIR : (t + 1) * PAIR]
+        found += [jnp.where(low, two, swap(two)), jnp.where(low, swap(two), two)]
     return found
-
-
-def swap(tile):
-    return jnp.concatenate([tile[:, BLK:], tile[:, :BLK]], axis=1)
 
 
 def masks_of(head, first, count, pairs):
     half = lax.broadcasted_iota(jnp.int32, (STEP, PAIR), 1) // BLK
     cols = [jnp.broadcast_to(head[:, first + n : first + n + 1], (STEP, PAIR)) for n in range(count)]
-    return [[(half + 2 * pair).astype(jnp.float32) == col for col in cols] for pair in pairs]
+    cols = [col.astype(jnp.int32).astype(jnp.int16) for col in cols]
+    return [[(half + 2 * pair).astype(jnp.int16) == col for col in cols] for pair in pairs]
 
 
 def source_of(shift, axis):
@@ -93,33 +90,25 @@
             for g in range(BLK // STEP):
                 copies_in = copies_of(held[place, n * BLK + g * STEP : n * BLK + (g + 1) * STEP, :])
                 for pair in range(NCC // 2):
-                    acc = jnp.where(masks[pair][0], copies_in[0], 0.0)
-                    for q in range(1, KP):
+                    acc = jnp.zeros((STEP, PAIR), jnp.bfloat16)
+                    for q in range(KP):
                         acc = jnp.where(masks[pair][q], copies_in[q], acc)
                     first = slab + g * STEP
-                    wide[first : first + STEP, pair * PAIR : (pair + 1) * PAIR] = acc.astype(jnp.bfloat16)
+                    wide[first : first + STEP, pair * PAIR : (pair + 1) * PAIR] = acc
 
 
 def gather_rows(a_ref, rows):
     sources = [source_of(shift, "row") for shifts in SHIFTS for shift in shifts]
-    half = lax.broadcasted_iota(jnp.int32, (STEP, PAIR), 1) // BLK
-    low = half.astype(jnp.int16) < jnp.int16(1)
     none = jnp.zeros((STEP, PAIR), jnp.bfloat16)
     for src in range(a_ref.shape[0]):
         head = a_ref[src, BODY:, :PAIR].astype(jnp.float32)
         for j in range(OWN):
             row = src * BLK
             for s in range(SEC):
-                at = (s * OWN + j) * KS
-                cols = [jnp.broadcast_to(head[:, at + k : at + k + 1], (STEP, PAIR)) for k in range(KS)]
-                cols = [col.astype(jnp.int32).astype(jnp.int16) for col in cols]
-                masks = [[(half + 2 * pair).astype(jnp.int16) == col for col in cols] for pair in sources]
+                masks = masks_of(head, (s * OWN + j) * KS, KS, sources)
                 for g in range(BLK // STEP):
                     first = (s * OWN + j) * BLK + g * STEP
-                    copies = []
-                    for t in range(KS // 2):
-                        two = a_ref[src, first : first + STEP, t * PAIR : (t + 1) * PAIR]
-                        copies += [jnp.where(low, two, swap(two)), jnp.where(low, swap(two), two)]
+                    copies = copies_of(a_ref[src, first : first + STEP, :])
                     for pair in range(IBS // OWN):
                         acc = jnp.where(masks[pair][0], copies[0], none)
                         for k in range(1, KS):
@@ -166,6 +155,7 @@
         out_shape=jax.ShapeDtypeStruct((BODY + HEAD, KP * BLK), jnp.bfloat16),
         in_specs=[SMEM, VMEM],
         out_specs=VMEM,
+        compiler_params=pltpu.CompilerParams(vmem_limit_bytes=SMALL),
     )(p_cols, p_blocks.reshape(BODY, KP * BLK))
 
     def expand(*parts):

time: 107 us -> 105 us (0.981)
  Pallas kernels: 14.4 us -> 12.9 us
  transfers between devices with their start and end apart: 7 -> 7, of which waited for: 3 -> 3; matrix products, arithmetic and copies ran while one was open for 0% -> 0% of each run, Pallas kernels for 6% -> 5%
where the time goes in v2:
time: 105 us
  blocking collectives  44 us (42%)
  starting transfers between devices  29 us (28%)
  waiting for transfers between devices  18.1 us (17%)
  Pallas kernels  12.9 us (12%)
    all_to_all x1, blocking collectives, local(): got = lax.all_to_all(part, 'layer', 0, 0, axis_index_groups=far, tiled=True)  25 us
    all_to_all x1, blocking collectives, local(): a_own = lax.all_to_all(a_out, 'chip', 0, 0, tiled=True)  19 us
    ppermute x3, starting transfers between devices, local(): sums.append(lax.ppermute(sent, ('core', 'layer'), partners(turn)))  15.7 us
    ppermute x3, waiting for transfers between devices, local(): sums.append(lax.ppermute(sent, ('core', 'layer'), partners(turn)))  12.4 us
    ppermute x3, starting transfers between devices, local(): lax.ppermute(p_out, 'row', [(i, (i + d) % rows) for i in range(rows)])  9.33 us
    pallas_call x4, Pallas kernels, product(): pl.pallas_call(lambda *refs: product_kernel(near, turn, *refs), out_shape...  6.37 us
    ppermute x3, waiting for transfers between devices, local(): lax.ppermute(p_out, 'row', [(i, (i + d) % rows) for i in range(rows)])  5.74 us
    ppermute x1, starting transfers between devices, local(): a_other = lax.ppermute(a_own, 'core', [(0, 1), (1, 0)])  4 us
  transfers between devices with their start and end apart: 7, of which 3 were waited for; matrix products, arithmetic and copies ran while one was open for 0% of the time, Pallas kernels for 5%

profile of v2, /device:TPU:33, one launch (start us, length us, event | category | flops | bytes accessed | tf_op | source)
XLA Modules:
  0.0 104.9 jit_solution(7152775843794905390)
XLA Ops:
  0.0 2.0 %shard_map.55 = bf16[4,272,512]{2,1,0:T(8,128)(2,1)} custom-call(s32[1,2,2,8]{3,2,1,0:T(2,128)} %a_cols.1, bf16[256,512]{1,0:T(8,128)(2,1)} %bitcast.9), custom_call_target="tpu_custom_call" | custom-call | tf_op jit(solution)/shard_map/pallas_call | solution.py:147
  2.0 19.0 %all_to_all.10.a_ref = bf16[4,272,512]{2,1,0:T(8,128)(2,1)S(1)} all-to-all(bf16[4,272,512]{2,1,0:T(8,128)(2,1)} %shard_map.55), channel_id=1, replica_groups=mesh['row'=4,'chip'=4,'core'=2,'layer'=16] {'chip'}, dimensions={0} | all-to-all | bytes 2228224 | tf_op jit(solution)/shard_map/all_to_all | solution.py:175
  21.0 4.0 %collective-permute-start = (bf16[4,272,512]{2,1,0:T(8,128)(2,1)S(1)}, bf16[4,272,512]{2,1,0:T(8,128)(2,1)S(1)}, u32[]{:S(2)}, u32[]{:S(2)}) collective-permute-start(bf16[4,272,512]{2,1,0:T(8,128)(2,1)S(1)} %all_to_all.10.a_ref), channel_id=1, source_target_pairs={{0,16},{16,0},{1,17},{17,1},{2,18},{18,2},{3,19},{19,3},{4,20},{20... | collective-permute-start | bytes 3342344 | tf_op jit(solution)/shard_map/ppermute | solution.py:178
  25.0 0.0 copy-done
  25.0 0.0 copy-done.2
  25.0 0.6 shard_map.58.refs_0_
  25.6 4.4 %collective-permute-start.1 = (bf16[272,256]{1,0:T(8,128)(2,1)S(1)}, bf16[272,256]{1,0:T(8,128)(2,1)S(1)}, u32[]{:S(2)}, u32[]{:S(2)}) collective-permute-start(bf16[272,256]{1,0:T(8,128)(2,1)S(1)} %shard_map.58.refs_0_), channel_id=1, source_target_pairs={{0,384},{128,0},{256,128},{384,256},{1,385},{129,1},{257,129},{385... | collective-permute-start | bytes 417800 | tf_op jit(solution)/shard_map/ppermute | solution.py:176
  30.0 2.4 %collective-permute-start.2 = (bf16[272,256]{1,0:T(8,128)(2,1)S(1)}, bf16[272,256]{1,0:T(8,128)(2,1)S(1)}, u32[]{:S(2)}, u32[]{:S(2)}) collective-permute-start(bf16[272,256]{1,0:T(8,128)(2,1)S(1)} %shard_map.58.refs_0_), channel_id=1, source_target_pairs={{0,256},{128,384},{256,0},{384,128},{1,257},{129,385},{257,1},{385... | collective-permute-start | bytes 417800 | tf_op jit(solution)/shard_map/ppermute | solution.py:176
  32.4 2.5 %collective-permute-start.3 = (bf16[272,256]{1,0:T(8,128)(2,1)S(1)}, bf16[272,256]{1,0:T(8,128)(2,1)S(1)}, u32[]{:S(2)}, u32[]{:S(2)}) collective-permute-start(bf16[272,256]{1,0:T(8,128)(2,1)S(1)} %shard_map.58.refs_0_), channel_id=1, source_target_pairs={{0,128},{128,256},{256,384},{384,0},{1,129},{129,257},{257,385},{3... | collective-permute-start | bytes 417800 | tf_op jit(solution)/shard_map/ppermute | solution.py:176
  35.0 0.0 collective-permute-done.1.refs_1_
  35.0 0.9 shard_map.59.refs_2_
  35.9 2.5 %collective-permute-done.2.refs_0_ = bf16[272,256]{1,0:T(8,128)(2,1)S(1)} collective-permute-done((bf16[272,256]{1,0:T(8,128)(2,1)S(1)}, bf16[272,256]{1,0:T(8,128)(2,1)S(1)}, u32[]{:S(2)}, u32[]{:S(2)}) %collective-permute-start.2) | collective-permute-done | bytes 139296 | tf_op jit(solution)/shard_map/ppermute | solution.py:176
  38.3 3.3 %collective-permute-done.3.refs_1_ = bf16[272,256]{1,0:T(8,128)(2,1)S(1)} collective-permute-done((bf16[272,256]{1,0:T(8,128)(2,1)S(1)}, bf16[272,256]{1,0:T(8,128)(2,1)S(1)}, u32[]{:S(2)}, u32[]{:S(2)}) %collective-permute-start.3) | collective-permute-done | bytes 139296 | tf_op jit(solution)/shard_map/ppermute | solution.py:176
  41.6 0.9 shard_map.60.refs_3_
  42.5 1.1 %shard_map.56.rows_own = bf16[2,256,1024]{2,1,0:T(8,128)(2,1)S(1)} custom-call(bf16[4,272,512]{2,1,0:T(8,128)(2,1)S(1)} %all_to_all.10.a_ref), custom_call_target="tpu_custom_call" | custom-call | flops 1000000 | bytes 2000000 | tf_op jit(solution)/shard_map/pallas_call | solution.py:179
  43.5 0.0 copy-start.1
  43.5 0.0 collective-permute-done.a_other
  43.6 1.1 %shard_map.57.refs_1_ = bf16[2,2,256,1024]{3,2,1,0:T(8,128)(2,1)S(1)} custom-call(bf16[2,256,1024]{2,1,0:T(8,128)(2,1)S(1)} %shard_map.56.rows_own, bf16[4,272,512]{2,1,0:T(8,128)(2,1)S(1)} %collective-permute-done.a_other), custom_call_target="tpu_custom_call" | custom-call | flops 1000000 | bytes 4000000 | tf_op jit(solution)/shard_map/pallas_call | solution.py:188
  44.6 0.0 copy-done.1
  44.7 1.6 %shard_map.63 = bf16[4,64,512]{2,1,0:T(8,128)(2,1)S(1)} custom-call(s32[1,8,16]{2,1,0:T(8,128)S(1)} %bitcast.5, bf16[2,2,256,1024]{3,2,1,0:T(8,128)(2,1)S(1)} %shard_map.57.refs_1_, bf16[512,1024]{1,0:T(8,128)(2,1)S(1)} %shard_map.59.refs_2_, bf16[512,1024]{1,0:T(8,128)(2,1)S(1)} %shard_map.60.refs_3_), custom_call_target="tpu_custom_call" | custom-call | flops 500000000 | bytes 3000000 | tf_op jit(solution)/shard_map/pallas_call | solution.py:198
  46.2 1.6 %shard_map.62 = bf16[4,64,512]{2,1,0:T(8,128)(2,1)S(1)} custom-call(s32[1,8,16]{2,1,0:T(8,128)S(1)} %bitcast.6, bf16[2,2,256,1024]{3,2,1,0:T(8,128)(2,1)S(1)} %shard_map.57.refs_1_, bf16[512,1024]{1,0:T(8,128)(2,1)S(1)} %shard_map.59.refs_2_, bf16[512,1024]{1,0:T(8,128)(2,1)S(1)} %shard_map.60.refs_3_), custom_call_target="tpu_custom_call" | custom-call | flops 500000000 | bytes 3000000 | tf_op jit(solution)/shard_map/pallas_call | solution.py:198
  47.8 1.6 %shard_map.61 = bf16[4,64,512]{2,1,0:T(8,128)(2,1)S(1)} custom-call(s32[1,8,16]{2,1,0:T(8,128)S(1)} %bitcast.7, bf16[2,2,256,1024]{3,2,1,0:T(8,128)(2,1)S(1)} %shard_map.57.refs_1_, bf16[512,1024]{1,0:T(8,128)(2,1)S(1)} %shard_map.59.refs_2_, bf16[512,1024]{1,0:T(8,128)(2,1)S(1)} %shard_map.60.refs_3_), custom_call_target="tpu_custom_call" | custom-call | flops 500000000 | bytes 3000000 | tf_op jit(solution)/shard_map/pallas_call | solution.py:198
  49.4 1.9 %collective-permute-start.6 = (bf16[4,64,512]{2,1,0:T(8,128)(2,1)S(1)}, bf16[4,64,512]{2,1,0:T(8,128)(2,1)S(1)}, u32[]{:S(2)}, u32[]{:S(2)}) collective-permute-start(bf16[4,64,512]{2,1,0:T(8,128)(2,1)S(1)} %shard_map.63), channel_id=1, source_target_pairs={{0,1},{1,0},{2,3},{3,2},{4,5},{5,4},{6,7},{7,6},{8,9},{9,8},{10,11... | collective-permute-start | bytes 786440 | tf_op jit(solution)/shard_map/ppermute | solution.py:220
  51.4 11.4 %collective-permute-start.5 = (bf16[4,64,512]{2,1,0:T(8,128)(2,1)S(1)}, bf16[4,64,512]{2,1,0:T(8,128)(2,1)S(1)}, u32[]{:S(2)}, u32[]{:S(2)}) collective-permute-start(bf16[4,64,512]{2,1,0:T(8,128)(2,1)S(1)} %shard_map.62), channel_id=1, source_target_pairs={{0,2},{1,3},{2,0},{3,1},{4,6},{5,7},{6,4},{7,5},{8,10},{9,11},{10,... | collective-permute-start | bytes 786440 | tf_op jit(solution)/shard_map/ppermute | solution.py:220
  62.8 2.4 %collective-permute-start.4 = (bf16[4,64,512]{2,1,0:T(8,128)(2,1)S(1)}, bf16[4,64,512]{2,1,0:T(8,128)(2,1)S(1)}, u32[]{:S(2)}, u32[]{:S(2)}) collective-permute-start(bf16[4,64,512]{2,1,0:T(8,128)(2,1)S(1)} %shard_map.61), channel_id=1, source_target_pairs={{0,3},{1,2},{2,1},{3,0},{4,7},{5,6},{6,5},{7,4},{8,11},{9,10},{10,... | collective-permute-start | bytes 786440 | tf_op jit(solution)/shard_map/ppermute | solution.py:220
  65.1 1.6 %shard_map.64 = bf16[4,64,512]{2,1,0:T(8,128)(2,1)S(1)} custom-call(s32[1,8,16]{2,1,0:T(8,128)S(1)} %bitcast.8, bf16[2,2,256,1024]{3,2,1,0:T(8,128)(2,1)S(1)} %shard_map.57.refs_1_, bf16[512,1024]{1,0:T(8,128)(2,1)S(1)} %shard_map.59.refs_2_, bf16[512,1024]{1,0:T(8,128)(2,1)S(1)} %shard_map.60.refs_3_), custom_call_target="tpu_custom_call" | custom-call | flops 500000000 | bytes 3000000 | tf_op jit(solution)/shard_map/pallas_call | solution.py:198
  66.7 0.0 collective-permute-done.6
  66.8 0.0 collective-permute-done.5
  66.8 12.4 %collective-permute-done.4 = bf16[4,64,512]{2,1,0:T(8,128)(2,1)S(1)} collective-permute-done((bf16[4,64,512]{2,1,0:T(8,128)(2,1)S(1)}, bf16[4,64,512]{2,1,0:T(8,128)(2,1)S(1)}, u32[]{:S(2)}, u32[]{:S(2)}) %collective-permute-start.4) | collective-permute-done | bytes 262176 | tf_op jit(solution)/shard_map/ppermute | solution.py:220
  79.1 0.1 add_convert_fusion
  79.3 25.0 %all_to_all.11 = bf16[4,64,512]{2,1,0:T(8,128)(2,1)S(1)} all-to-all(bf16[4,64,512]{2,1,0:T(8,128)(2,1)S(1)} %add_convert_fusion), channel_id=1, replica_groups={{0,4,8,12},{1,5,9,13},{2,6,10,14},{3,7,11,15},{16,20,24,28},{17,21,25,2..., dimensions={0} | all-to-all | bytes 524288 | tf_op jit(solution)/shard_map/all_to_all | solution.py:224
  104.3 0.7 reduce_sum.12
  (2 shorter events, 0.0 us)
Async XLA Ops:
  2.0 23.0 %copy-start = (bf16[1,2,1,2,64,256]{5,4,3,2,1,0:T(8,128)(2,1)S(1)}, bf16[1,2,1,2,64,256]{5,4,3,2,1,0:T(8,128)(2,1)}, u32[]{:S(2)}) copy-start(bf16[1,2,1,2,64,256]{5,4,3,2,1,0:T(8,128)(2,1)} %param.7) | copy-start | bytes 393220
  2.0 23.0 %copy-start.2 = (s32[1,2,1,2,4]{4,3,2,1,0:T(2,128)S(1)}, s32[1,2,1,2,4]{4,3,2,1,0:T(2,128)}, u32[]{:S(2)}) copy-start(s32[1,2,1,2,4]{4,3,2,1,0:T(2,128)} %p_cols.1) | copy-start | bytes 196
  21.0 22.6 %collective-permute-start = (bf16[4,272,512]{2,1,0:T(8,128)(2,1)S(1)}, bf16[4,272,512]{2,1,0:T(8,128)(2,1)S(1)}, u32[]{:S(2)}, u32[]{:S(2)}) collective-permute-start(bf16[4,272,512]{2,1,0:T(8,128)(2,1)S(1)} %all_to_all.10.a_ref), channel_id=1, source_target_pairs={{0,16},{16,0},{1,17},{17,1},{2,18},{18,2},{3,19},{19,3},{4,20},{20... | collective-permute-start | bytes 3342344 | tf_op jit(solution)/shard_map/ppermute | solution.py:178
  25.6 9.4 %collective-permute-start.1 = (bf16[272,256]{1,0:T(8,128)(2,1)S(1)}, bf16[272,256]{1,0:T(8,128)(2,1)S(1)}, u32[]{:S(2)}, u32[]{:S(2)}) collective-permute-start(bf16[272,256]{1,0:T(8,128)(2,1)S(1)} %shard_map.58.refs_0_), channel_id=1, source_target_pairs={{0,384},{128,0},{256,128},{384,256},{1,385},{129,1},{257,129},{385... | collective-permute-start | bytes 417800 | tf_op jit(solution)/shard_map/ppermute | solution.py:176
  30.0 8.3 %collective-permute-start.2 = (bf16[272,256]{1,0:T(8,128)(2,1)S(1)}, bf16[272,256]{1,0:T(8,128)(2,1)S(1)}, u32[]{:S(2)}, u32[]{:S(2)}) collective-permute-start(bf16[272,256]{1,0:T(8,128)(2,1)S(1)} %shard_map.58.refs_0_), channel_id=1, source_target_pairs={{0,256},{128,384},{256,0},{384,128},{1,257},{129,385},{257,1},{385... | collective-permute-start | bytes 417800 | tf_op jit(solution)/shard_map/ppermute | solution.py:176
  32.4 9.2 %collective-permute-start.3 = (bf16[272,256]{1,0:T(8,128)(2,1)S(1)}, bf16[272,256]{1,0:T(8,128)(2,1)S(1)}, u32[]{:S(2)}, u32[]{:S(2)}) collective-permute-start(bf16[272,256]{1,0:T(8,128)(2,1)S(1)} %shard_map.58.refs_0_), channel_id=1, source_target_pairs={{0,128},{128,256},{256,384},{384,0},{1,129},{129,257},{257,385},{3... | collective-permute-start | bytes 417800 | tf_op jit(solution)/shard_map/ppermute | solution.py:176
  43.5 1.1 %copy-start.1 = (s32[1,16,8]{1,2,0:T(8,128)S(1)}, s32[1,16,8]{1,2,0:T(8,128)}, u32[]{:S(2)}) copy-start(s32[1,16,8]{1,2,0:T(8,128)} %param.9) | copy-start | bytes 1540
  49.4 17.3 %collective-permute-start.6 = (bf16[4,64,512]{2,1,0:T(8,128)(2,1)S(1)}, bf16[4,64,512]{2,1,0:T(8,128)(2,1)S(1)}, u32[]{:S(2)}, u32[]{:S(2)}) collective-permute-start(bf16[4,64,512]{2,1,0:T(8,128)(2,1)S(1)} %shard_map.63), channel_id=1, source_target_pairs={{0,1},{1,0},{2,3},{3,2},{4,5},{5,4},{6,7},{7,6},{8,9},{9,8},{10,11... | collective-permute-start | bytes 786440 | tf_op jit(solution)/shard_map/ppermute | solution.py:220
  51.4 15.4 %collective-permute-start.5 = (bf16[4,64,512]{2,1,0:T(8,128)(2,1)S(1)}, bf16[4,64,512]{2,1,0:T(8,128)(2,1)S(1)}, u32[]{:S(2)}, u32[]{:S(2)}) collective-permute-start(bf16[4,64,512]{2,1,0:T(8,128)(2,1)S(1)} %shard_map.62), channel_id=1, source_target_pairs={{0,2},{1,3},{2,0},{3,1},{4,6},{5,7},{6,4},{7,5},{8,10},{9,11},{10,... | collective-permute-start | bytes 786440 | tf_op jit(solution)/shard_map/ppermute | solution.py:220
  62.8 16.4 %collective-permute-start.4 = (bf16[4,64,512]{2,1,0:T(8,128)(2,1)S(1)}, bf16[4,64,512]{2,1,0:T(8,128)(2,1)S(1)}, u32[]{:S(2)}, u32[]{:S(2)}) collective-permute-start(bf16[4,64,512]{2,1,0:T(8,128)(2,1)S(1)} %shard_map.61), channel_id=1, source_target_pairs={{0,3},{1,2},{2,1},{3,0},{4,7},{5,6},{6,5},{7,4},{8,11},{9,10},{10,... | collective-permute-start | bytes 786440 | tf_op jit(solution)/shard_map/ppermute | solution.py:220
